TPU v7x, 32 devices: a whole 2x2x4 slice. The times are simulated.
32 devices in a mesh: group: 2 (over y), quad: 2 (over core), rows: 8 (over z, x).
Axes of the slice: x: 2, y: 2, z: 4, core: 2. Of those that a mesh axis runs over, the one named last changes fastest.
Arguments:
- solutions: bfloat16 [32, 20480, 128], P('quad', ('group', 'rows')), parts along dimension 1, may hold values from -24 to 24
- point_of_slot: int32 [64], P(('group', 'quad')), parts along dimension 0, may hold values from 0 to 31, each once
- mass_blocks: bfloat16 [160, 20, 128, 128], P(('group', 'rows')), parts along dimension 0, may hold values from -0.125 to 0.125
- block_cols: int32 [160, 20], P(('group', 'rows')), parts along dimension 0, may hold values from 0 to 79, as said below
- sources: bfloat16 [20480, 64], P(('group', 'rows')), parts along dimension 0, may hold values from -0.0625 to 0.0625
Outputs:
- mass_applied: bfloat16 [8, 20480, 128], P('quad', ('group', 'rows')), parts along dimension 1
- reduced: float32 [16, 64, 128], P(('group', 'quad')), parts along dimension 0
There are 2 independent parts, one for each index of `group`. A program takes and returns all parts, laid end to end along the dimension named above; each array names one. Nothing has to cross between parts.
Inputs may be any that keep to these rules, and one draw needn't show every extreme that they name: `point_of_slot`: each contour point sits in exactly one slot. `block_cols`: slot 0 of block row i holds i; every entry c of block row i has |c - i| <= 10; entries of a block row may repeat.
All inputs are finite; a program needn't handle non-finite values.
Results may differ from a plain program's by a relative error of at most 0.0063.
Values may be sent and summed in bfloat16 or wider, within the bound.
A program may use at most 128 MiB of HBM per device.

v0:
```python
import math
import jax
import jax.numpy as jnp
from jax import lax
from jax.sharding import PartitionSpec as P

MOMENTS = 8


def with_halo(block, sides, width):
    for axis, dim in sides:
        count = lax.axis_size(axis)
        forward = [(i, i + 1) for i in range(count - 1)]
        backward = [(target, source) for source, target in forward]
        low = lax.ppermute(
            lax.slice_in_dim(block, block.shape[dim] - width, None, axis=dim), axis, forward
        )
        high = lax.ppermute(lax.slice_in_dim(block, 0, width, axis=dim), axis, backward)
        block = jnp.concatenate([low, block, high], axis=dim)
    return block


def local(solutions, point_of_slot, mass_blocks, block_cols, sources):
    local_points = solutions.shape[0]
    rows_here = solutions.shape[1]
    width = solutions.shape[2] // 2
    block_size = mass_blocks.shape[2]
    span_blocks = rows_here // block_size
    total_points = local_points * lax.axis_size("quad")
    theta = 2.0 * math.pi * (point_of_slot.astype(jnp.float32) + 0.5) / total_points
    powers = jnp.arange(1, MOMENTS + 1, dtype=jnp.float32)
    angles = powers[:, None] * theta[None, :]
    cosine = (jnp.cos(angles) / total_points).astype(jnp.bfloat16)
    sine = (jnp.sin(angles) / total_points).astype(jnp.bfloat16)
    weighting = jnp.concatenate(
        [jnp.concatenate([cosine, -sine], axis=1), jnp.concatenate([sine, cosine], axis=1)], axis=0
    )
    stacked = jnp.concatenate([solutions[:, :, :width], solutions[:, :, width:]], axis=0).reshape(
        2 * local_points, rows_here * width
    )
    product = jnp.dot(weighting, stacked, preferred_element_type=jnp.float32).reshape(
        2, MOMENTS, rows_here, width
    )
    partial_value = jnp.concatenate([product[0], product[1]], axis=2)
    summed = lax.psum_scatter(
        partial_value.astype(jnp.bfloat16), "quad", scatter_dimension=0, tiled=True
    )
    widened = with_halo(summed, (("rows", 1),), rows_here)
    owned = widened.shape[0]
    panel_blocks = widened.reshape(owned, 3 * span_blocks, block_size, 2 * width)
    offset = (lax.axis_index("rows") - 1) * span_blocks
    local_cols = block_cols - offset

    def add_slot(slot_index, accum):
        columns_now = lax.dynamic_index_in_dim(local_cols, slot_index, 1, keepdims=False)
        tiles = lax.dynamic_index_in_dim(mass_blocks, slot_index, 1, keepdims=False)
        chosen = jnp.take(panel_blocks, columns_now, axis=1)
        return accum + jnp.einsum(
            "bij,mbjc->mbic", tiles, chosen, preferred_element_type=jnp.float32
        )

    start = jnp.zeros((owned, span_blocks, block_size, 2 * width), jnp.float32)
    accum = lax.fori_loop(0, mass_blocks.shape[1], add_slot, start)
    mass_applied = accum.astype(jnp.bfloat16).reshape(owned, rows_here, 2 * width)
    term = jnp.einsum("nl,mnc->mlc", sources, mass_applied, preferred_element_type=jnp.float32)
    reduced = lax.psum(term, "rows")
    return (mass_applied, reduced)


def solution(mesh):
    in_specs = (
        P("quad", ("group", "rows"), None),
        P(("group", "quad")),
        P(("group", "rows"), None, None, None),
        P(("group", "rows"), None),
        P(("group", "rows"), None),
    )
    out_specs = (P("quad", ("group", "rows"), None), P(("group", "quad"), None, None))
    return jax.shard_map(local, mesh=mesh, in_specs=in_specs, out_specs=out_specs, check_vma=False)
```

profile of v0, /device:TPU:0, one launch (start us, length us, event | category | flops | bytes accessed | tf_op | source)
XLA Modules:
  0.0 360.4 jit_solution(8767919289996625870)
XLA Ops:
  8.2 9.6 %fusion.22 = (bf16[16,1280,64]{2,1,0:T(8,128)(2,1)}, bf16[16,1280,64]{2,1,0:T(8,128)(2,1)}) fusion(bf16[16,1280,128]{2,1,0:T(8,128)(2,1)} %param.7), kind=kLoop, calls=%fused_computation.37 | loop fusion | bytes 10485760 | tf_op jit(solution)/shard_map/slice | solution.py:38
  17.8 10.4 %pad_maximum_fusion = bf16[32,1280,64]{2,1,0:T(8,128)(2,1)} fusion(bf16[16,1280,64]{2,1,0:T(8,128)(2,1)} %get-tuple-element.138, bf16[16,1280,64]{2,1,0:T(8,128)(2,1)} %get-tuple-element.137), kind=kLoop, calls=%fused_computation.14 | loop fusion | flops 2621440 | bytes 10485760 | tf_op jit(solution)/shard_map/concatenate | solution.py:38
  28.2 11.0 %reshape.29 = bf16[32,81920]{1,0:T(8,128)(2,1)} reshape(bf16[32,1280,64]{2,1,0:T(8,128)(2,1)} %pad_maximum_fusion) | data formatting | bytes 10485760 | tf_op jit(solution)/shard_map/reshape | solution.py:38
  39.2 3.4 convolution_convert_fusion
  45.5 3.1 squeeze.20
  48.6 3.0 reshape.45
  51.6 4.3 %squeeze.21 = bf16[8,1280,64]{2,1,0:T(8,128)(2,1)} reshape(bf16[655360]{0:T(1024)(128)(2,1)} %reshape.45) | data formatting | bytes 2621440 | tf_op jit(solution)/shard_map/squeeze | solution.py:44
  55.9 4.7 %pad_maximum_fusion.2 = bf16[8,1280,128]{2,1,0:T(8,128)(2,1)} fusion(bf16[8,1280,64]{2,1,0:T(8,128)(2,1)} %squeeze.21, bf16[8,1280,64]{2,1,0:T(8,128)(2,1)S(1)} %squeeze.20), kind=kLoop, calls=%fused_computation.16 | loop fusion | flops 5242880 | bytes 5242880 | tf_op jit(solution)/shard_map/concatenate | solution.py:44
  60.6 13.0 %reduce-scatter.2.cloned.1.call-done = bf16[4,1280,128]{2,1,0:T(8,128)(2,1)} async-done(((bf16[8,1280,128]{2,1,0:T(8,128)(2,1)}), bf16[4,1280,128]{2,1,0:T(8,128)(2,1)}) %reduce-scatter.2.cloned.1.call-update) | async-done | bytes 1310736 | tf_op jit(solution)/shard_map/reduce_scatter | solution.py:45
  73.6 3.8 %collective-permute-start = (bf16[4,1280,128]{2,1,0:T(8,128)(2,1)}, bf16[4,1280,128]{2,1,0:T(8,128)(2,1)S(1)}, u32[]{:S(2)}, u32[]{:S(2)}) collective-permute-start(bf16[4,1280,128]{2,1,0:T(8,128)(2,1)} %reduce-scatter.2.cloned.1.call-done), channel_id=1, source_target_pairs={{0,1},{1,2},{2,3},{3,4},{4,5},{5,6},{6,7},{8,9},{9,10},{10,11},{11... | collective-permute-start | bytes 3932168 | tf_op jit(solution)/shard_map/ppermute | solution.py:15
  78.8 55.3 %collective-permute-done = bf16[4,1280,128]{2,1,0:T(8,128)(2,1)S(1)} collective-permute-done((bf16[4,1280,128]{2,1,0:T(8,128)(2,1)}, bf16[4,1280,128]{2,1,0:T(8,128)(2,1)S(1)}, u32[]{:S(2)}, u32[]{:S(2)}) %collective-permute-start) | collective-permute-done | bytes 1310752 | tf_op jit(solution)/shard_map/ppermute | solution.py:15
  134.1 3.1 pad_maximum_fusion.1
  137.2 139.2 %while.14 = (s32[]{:T(128)}, f32[4,10,128,128]{2,3,0,1:T(8,128)}, s32[10,20]{0,1:T(8,128)S(1)}, bf16[4,30,128,128]{3,2,1,0:T(8,128)(2,1)}, bf16[10,20,128,128]{3,2,1,0:T(8,128)(2,1)}, /*index=5*/s32[]{:T(128)}, s32[]{:T(128)}) while((s32[]{:T(128)}, f32[4,10,128,128]{2,3,0,1:T(8,128)}, s32[10,20]{0,1:T(8,128)S(1)}, ...), condition=%wide.region_2.3_spmd.clone, body=%wide.region_1.2_spmd.clone.sunk | while | flops 169739328 | bytes 9507599 | solution.py:63
  137.2 2.9 gather_fusion
  140.2 3.2 bitcast_add_fusion.2
  143.4 2.9 gather_fusion
  146.3 4.1 %bitcast_add_fusion.2 = f32[4,10,128,128]{2,3,0,1:T(8,128)} fusion(f32[4,10,128,128]{2,3,0,1:T(8,128)} %get-tuple-element.186, bf16[10,4,128,128]{3,2,1,0:T(8,128)(2,1)S(1)} %gather_fusion, pred[10]{0:T(512)(128)(4,1)S(1)} %get-tuple-element.177, pred[]{:T(512)S(6)} %compare.3, bf16[10,20,128,128]{3,2,1,0:T(8,128)(2,1)} %get-tuple-element.196, ...), kind=kOutput, calls=%fused_computation.1.clone.1 | convolution fusion | flops 169738240 | bytes 6881803 | tf_op jit(solution)/shard_map/while/body/eval_jaxpr/bij,mbjc->mbic/dot_general | solution.py:58
  150.4 2.9 gather_fusion
  153.3 4.1 %bitcast_add_fusion.2 = f32[4,10,128,128]{2,3,0,1:T(8,128)} fusion(f32[4,10,128,128]{2,3,0,1:T(8,128)} %get-tuple-element.186, bf16[10,4,128,128]{3,2,1,0:T(8,128)(2,1)S(1)} %gather_fusion, pred[10]{0:T(512)(128)(4,1)S(1)} %get-tuple-element.177, pred[]{:T(512)S(6)} %compare.3, bf16[10,20,128,128]{3,2,1,0:T(8,128)(2,1)} %get-tuple-element.196, ...), kind=kOutput, calls=%fused_computation.1.clone.1 | convolution fusion | flops 169738240 | bytes 6881803 | tf_op jit(solution)/shard_map/while/body/eval_jaxpr/bij,mbjc->mbic/dot_general | solution.py:58
  157.4 2.9 gather_fusion
  160.3 4.1 %bitcast_add_fusion.2 = f32[4,10,128,128]{2,3,0,1:T(8,128)} fusion(f32[4,10,128,128]{2,3,0,1:T(8,128)} %get-tuple-element.186, bf16[10,4,128,128]{3,2,1,0:T(8,128)(2,1)S(1)} %gather_fusion, pred[10]{0:T(512)(128)(4,1)S(1)} %get-tuple-element.177, pred[]{:T(512)S(6)} %compare.3, bf16[10,20,128,128]{3,2,1,0:T(8,128)(2,1)} %get-tuple-element.196, ...), kind=kOutput, calls=%fused_computation.1.clone.1 | convolution fusion | flops 169738240 | bytes 6881803 | tf_op jit(solution)/shard_map/while/body/eval_jaxpr/bij,mbjc->mbic/dot_general | solution.py:58
  164.4 2.9 gather_fusion
  167.3 4.1 %bitcast_add_fusion.2 = f32[4,10,128,128]{2,3,0,1:T(8,128)} fusion(f32[4,10,128,128]{2,3,0,1:T(8,128)} %get-tuple-element.186, bf16[10,4,128,128]{3,2,1,0:T(8,128)(2,1)S(1)} %gather_fusion, pred[10]{0:T(512)(128)(4,1)S(1)} %get-tuple-element.177, pred[]{:T(512)S(6)} %compare.3, bf16[10,20,128,128]{3,2,1,0:T(8,128)(2,1)} %get-tuple-element.196, ...), kind=kOutput, calls=%fused_computation.1.clone.1 | convolution fusion | flops 169738240 | bytes 6881803 | tf_op jit(solution)/shard_map/while/body/eval_jaxpr/bij,mbjc->mbic/dot_general | solution.py:58
  171.4 2.9 gather_fusion
  174.3 4.1 %bitcast_add_fusion.2 = f32[4,10,128,128]{2,3,0,1:T(8,128)} fusion(f32[4,10,128,128]{2,3,0,1:T(8,128)} %get-tuple-element.186, bf16[10,4,128,128]{3,2,1,0:T(8,128)(2,1)S(1)} %gather_fusion, pred[10]{0:T(512)(128)(4,1)S(1)} %get-tuple-element.177, pred[]{:T(512)S(6)} %compare.3, bf16[10,20,128,128]{3,2,1,0:T(8,128)(2,1)} %get-tuple-element.196, ...), kind=kOutput, calls=%fused_computation.1.clone.1 | convolution fusion | flops 169738240 | bytes 6881803 | tf_op jit(solution)/shard_map/while/body/eval_jaxpr/bij,mbjc->mbic/dot_general | solution.py:58
  178.4 2.9 gather_fusion
  181.3 4.1 %bitcast_add_fusion.2 = f32[4,10,128,128]{2,3,0,1:T(8,128)} fusion(f32[4,10,128,128]{2,3,0,1:T(8,128)} %get-tuple-element.186, bf16[10,4,128,128]{3,2,1,0:T(8,128)(2,1)S(1)} %gather_fusion, pred[10]{0:T(512)(128)(4,1)S(1)} %get-tuple-element.177, pred[]{:T(512)S(6)} %compare.3, bf16[10,20,128,128]{3,2,1,0:T(8,128)(2,1)} %get-tuple-element.196, ...), kind=kOutput, calls=%fused_computation.1.clone.1 | convolution fusion | flops 169738240 | bytes 6881803 | tf_op jit(solution)/shard_map/while/body/eval_jaxpr/bij,mbjc->mbic/dot_general | solution.py:58
  185.4 2.9 gather_fusion
  188.3 4.1 %bitcast_add_fusion.2 = f32[4,10,128,128]{2,3,0,1:T(8,128)} fusion(f32[4,10,128,128]{2,3,0,1:T(8,128)} %get-tuple-element.186, bf16[10,4,128,128]{3,2,1,0:T(8,128)(2,1)S(1)} %gather_fusion, pred[10]{0:T(512)(128)(4,1)S(1)} %get-tuple-element.177, pred[]{:T(512)S(6)} %compare.3, bf16[10,20,128,128]{3,2,1,0:T(8,128)(2,1)} %get-tuple-element.196, ...), kind=kOutput, calls=%fused_computation.1.clone.1 | convolution fusion | flops 169738240 | bytes 6881803 | tf_op jit(solution)/shard_map/while/body/eval_jaxpr/bij,mbjc->mbic/dot_general | solution.py:58
  192.4 2.9 gather_fusion
  195.3 4.1 %bitcast_add_fusion.2 = f32[4,10,128,128]{2,3,0,1:T(8,128)} fusion(f32[4,10,128,128]{2,3,0,1:T(8,128)} %get-tuple-element.186, bf16[10,4,128,128]{3,2,1,0:T(8,128)(2,1)S(1)} %gather_fusion, pred[10]{0:T(512)(128)(4,1)S(1)} %get-tuple-element.177, pred[]{:T(512)S(6)} %compare.3, bf16[10,20,128,128]{3,2,1,0:T(8,128)(2,1)} %get-tuple-element.196, ...), kind=kOutput, calls=%fused_computation.1.clone.1 | convolution fusion | flops 169738240 | bytes 6881803 | tf_op jit(solution)/shard_map/while/body/eval_jaxpr/bij,mbjc->mbic/dot_general | solution.py:58
  199.4 2.9 gather_fusion
  202.3 4.1 %bitcast_add_fusion.2 = f32[4,10,128,128]{2,3,0,1:T(8,128)} fusion(f32[4,10,128,128]{2,3,0,1:T(8,128)} %get-tuple-element.186, bf16[10,4,128,128]{3,2,1,0:T(8,128)(2,1)S(1)} %gather_fusion, pred[10]{0:T(512)(128)(4,1)S(1)} %get-tuple-element.177, pred[]{:T(512)S(6)} %compare.3, bf16[10,20,128,128]{3,2,1,0:T(8,128)(2,1)} %get-tuple-element.196, ...), kind=kOutput, calls=%fused_computation.1.clone.1 | convolution fusion | flops 169738240 | bytes 6881803 | tf_op jit(solution)/shard_map/while/body/eval_jaxpr/bij,mbjc->mbic/dot_general | solution.py:58
  206.4 2.9 gather_fusion
  209.3 4.1 %bitcast_add_fusion.2 = f32[4,10,128,128]{2,3,0,1:T(8,128)} fusion(f32[4,10,128,128]{2,3,0,1:T(8,128)} %get-tuple-element.186, bf16[10,4,128,128]{3,2,1,0:T(8,128)(2,1)S(1)} %gather_fusion, pred[10]{0:T(512)(128)(4,1)S(1)} %get-tuple-element.177, pred[]{:T(512)S(6)} %compare.3, bf16[10,20,128,128]{3,2,1,0:T(8,128)(2,1)} %get-tuple-element.196, ...), kind=kOutput, calls=%fused_computation.1.clone.1 | convolution fusion | flops 169738240 | bytes 6881803 | tf_op jit(solution)/shard_map/while/body/eval_jaxpr/bij,mbjc->mbic/dot_general | solution.py:58
  213.4 2.9 gather_fusion
  216.3 4.1 %bitcast_add_fusion.2 = f32[4,10,128,128]{2,3,0,1:T(8,128)} fusion(f32[4,10,128,128]{2,3,0,1:T(8,128)} %get-tuple-element.186, bf16[10,4,128,128]{3,2,1,0:T(8,128)(2,1)S(1)} %gather_fusion, pred[10]{0:T(512)(128)(4,1)S(1)} %get-tuple-element.177, pred[]{:T(512)S(6)} %compare.3, bf16[10,20,128,128]{3,2,1,0:T(8,128)(2,1)} %get-tuple-element.196, ...), kind=kOutput, calls=%fused_computation.1.clone.1 | convolution fusion | flops 169738240 | bytes 6881803 | tf_op jit(solution)/shard_map/while/body/eval_jaxpr/bij,mbjc->mbic/dot_general | solution.py:58
  220.4 2.9 gather_fusion
  223.4 4.1 %bitcast_add_fusion.2 = f32[4,10,128,128]{2,3,0,1:T(8,128)} fusion(f32[4,10,128,128]{2,3,0,1:T(8,128)} %get-tuple-element.186, bf16[10,4,128,128]{3,2,1,0:T(8,128)(2,1)S(1)} %gather_fusion, pred[10]{0:T(512)(128)(4,1)S(1)} %get-tuple-element.177, pred[]{:T(512)S(6)} %compare.3, bf16[10,20,128,128]{3,2,1,0:T(8,128)(2,1)} %get-tuple-element.196, ...), kind=kOutput, calls=%fused_computation.1.clone.1 | convolution fusion | flops 169738240 | bytes 6881803 | tf_op jit(solution)/shard_map/while/body/eval_jaxpr/bij,mbjc->mbic/dot_general | solution.py:58
  227.4 2.9 gather_fusion
  230.4 4.1 %bitcast_add_fusion.2 = f32[4,10,128,128]{2,3,0,1:T(8,128)} fusion(f32[4,10,128,128]{2,3,0,1:T(8,128)} %get-tuple-element.186, bf16[10,4,128,128]{3,2,1,0:T(8,128)(2,1)S(1)} %gather_fusion, pred[10]{0:T(512)(128)(4,1)S(1)} %get-tuple-element.177, pred[]{:T(512)S(6)} %compare.3, bf16[10,20,128,128]{3,2,1,0:T(8,128)(2,1)} %get-tuple-element.196, ...), kind=kOutput, calls=%fused_computation.1.clone.1 | convolution fusion | flops 169738240 | bytes 6881803 | tf_op jit(solution)/shard_map/while/body/eval_jaxpr/bij,mbjc->mbic/dot_general | solution.py:58
  237.4 4.1 %bitcast_add_fusion.2 = f32[4,10,128,128]{2,3,0,1:T(8,128)} fusion(f32[4,10,128,128]{2,3,0,1:T(8,128)} %get-tuple-element.186, bf16[10,4,128,128]{3,2,1,0:T(8,128)(2,1)S(1)} %gather_fusion, pred[10]{0:T(512)(128)(4,1)S(1)} %get-tuple-element.177, pred[]{:T(512)S(6)} %compare.3, bf16[10,20,128,128]{3,2,1,0:T(8,128)(2,1)} %get-tuple-element.196, ...), kind=kOutput, calls=%fused_computation.1.clone.1 | convolution fusion | flops 169738240 | bytes 6881803 | tf_op jit(solution)/shard_map/while/body/eval_jaxpr/bij,mbjc->mbic/dot_general | solution.py:58
  244.4 4.1 %bitcast_add_fusion.2 = f32[4,10,128,128]{2,3,0,1:T(8,128)} fusion(f32[4,10,128,128]{2,3,0,1:T(8,128)} %get-tuple-element.186, bf16[10,4,128,128]{3,2,1,0:T(8,128)(2,1)S(1)} %gather_fusion, pred[10]{0:T(512)(128)(4,1)S(1)} %get-tuple-element.177, pred[]{:T(512)S(6)} %compare.3, bf16[10,20,128,128]{3,2,1,0:T(8,128)(2,1)} %get-tuple-element.196, ...), kind=kOutput, calls=%fused_computation.1.clone.1 | convolution fusion | flops 169738240 | bytes 6881803 | tf_op jit(solution)/shard_map/while/body/eval_jaxpr/bij,mbjc->mbic/dot_general | solution.py:58
  251.4 4.1 %bitcast_add_fusion.2 = f32[4,10,128,128]{2,3,0,1:T(8,128)} fusion(f32[4,10,128,128]{2,3,0,1:T(8,128)} %get-tuple-element.186, bf16[10,4,128,128]{3,2,1,0:T(8,128)(2,1)S(1)} %gather_fusion, pred[10]{0:T(512)(128)(4,1)S(1)} %get-tuple-element.177, pred[]{:T(512)S(6)} %compare.3, bf16[10,20,128,128]{3,2,1,0:T(8,128)(2,1)} %get-tuple-element.196, ...), kind=kOutput, calls=%fused_computation.1.clone.1 | convolution fusion | flops 169738240 | bytes 6881803 | tf_op jit(solution)/shard_map/while/body/eval_jaxpr/bij,mbjc->mbic/dot_general | solution.py:58
  258.4 4.1 %bitcast_add_fusion.2 = f32[4,10,128,128]{2,3,0,1:T(8,128)} fusion(f32[4,10,128,128]{2,3,0,1:T(8,128)} %get-tuple-element.186, bf16[10,4,128,128]{3,2,1,0:T(8,128)(2,1)S(1)} %gather_fusion, pred[10]{0:T(512)(128)(4,1)S(1)} %get-tuple-element.177, pred[]{:T(512)S(6)} %compare.3, bf16[10,20,128,128]{3,2,1,0:T(8,128)(2,1)} %get-tuple-element.196, ...), kind=kOutput, calls=%fused_computation.1.clone.1 | convolution fusion | flops 169738240 | bytes 6881803 | tf_op jit(solution)/shard_map/while/body/eval_jaxpr/bij,mbjc->mbic/dot_general | solution.py:58
  265.4 4.1 %bitcast_add_fusion.2 = f32[4,10,128,128]{2,3,0,1:T(8,128)} fusion(f32[4,10,128,128]{2,3,0,1:T(8,128)} %get-tuple-element.186, bf16[10,4,128,128]{3,2,1,0:T(8,128)(2,1)S(1)} %gather_fusion, pred[10]{0:T(512)(128)(4,1)S(1)} %get-tuple-element.177, pred[]{:T(512)S(6)} %compare.3, bf16[10,20,128,128]{3,2,1,0:T(8,128)(2,1)} %get-tuple-element.196, ...), kind=kOutput, calls=%fused_computation.1.clone.1 | convolution fusion | flops 169738240 | bytes 6881803 | tf_op jit(solution)/shard_map/while/body/eval_jaxpr/bij,mbjc->mbic/dot_general | solution.py:58
  272.4 4.1 %bitcast_add_fusion.2 = f32[4,10,128,128]{2,3,0,1:T(8,128)} fusion(f32[4,10,128,128]{2,3,0,1:T(8,128)} %get-tuple-element.186, bf16[10,4,128,128]{3,2,1,0:T(8,128)(2,1)S(1)} %gather_fusion, pred[10]{0:T(512)(128)(4,1)S(1)} %get-tuple-element.177, pred[]{:T(512)S(6)} %compare.3, bf16[10,20,128,128]{3,2,1,0:T(8,128)(2,1)} %get-tuple-element.196, ...), kind=kOutput, calls=%fused_computation.1.clone.1 | convolution fusion | flops 169738240 | bytes 6881803 | tf_op jit(solution)/shard_map/while/body/eval_jaxpr/bij,mbjc->mbic/dot_general | solution.py:58
  280.3 71.7 %all-reduce.2.cloned.1.call-done = f32[4,64,128]{2,1,0:T(8,128)} async-done(((f32[4,64,128]{2,1,0:T(8,128)}), f32[4,64,128]{2,1,0:T(8,128)}) %all-reduce.2.cloned.1.call-update) | async-done | bytes 131088 | tf_op jit(solution)/shard_map/psum | solution.py:66
  (71 shorter events, 28.5 us)
Async XLA Ops:
  7.2 272.0 %copy-start = (bf16[1280,64]{0,1:T(8,128)(2,1)S(1)}, bf16[1280,64]{0,1:T(8,128)(2,1)}, u32[]{:S(2)}) copy-start(bf16[1280,64]{0,1:T(8,128)(2,1)} %param.11) | copy-start | bytes 491524
  7.2 66.4 %reduce-scatter.2.cloned.1.call-start = ((), (), s32[]{:S(2)}) async-start(), calls=%async_computation.1 | async-start | bytes 3932160 | tf_op jit(solution)/shard_map/reduce_scatter | solution.py:45
  60.6 18.2 %copy-start.2 = (s32[10,20]{1,0:T(8,128)S(1)}, s32[10,20]{1,0:T(8,128)}, u32[]{:S(2)}) copy-start(s32[10,20]{1,0:T(8,128)} %param.10) | copy-start | bytes 2404
  60.6 291.4 %all-reduce.2.cloned.1.call-start = ((), (), s32[]{:S(2)}) async-start(), calls=%async_computation.2 | async-start | bytes 262144 | tf_op jit(solution)/shard_map/psum | solution.py:66
  73.6 60.5 %collective-permute-start = (bf16[4,1280,128]{2,1,0:T(8,128)(2,1)}, bf16[4,1280,128]{2,1,0:T(8,128)(2,1)S(1)}, u32[]{:S(2)}, u32[]{:S(2)}) collective-permute-start(bf16[4,1280,128]{2,1,0:T(8,128)(2,1)} %reduce-scatter.2.cloned.1.call-done), channel_id=1, source_target_pairs={{0,1},{1,2},{2,3},{3,4},{4,5},{5,6},{6,7},{8,9},{9,10},{10,11},{11... | collective-permute-start | bytes 3932168 | tf_op jit(solution)/shard_map/ppermute | solution.py:15
  77.4 56.7 %collective-permute-start.1 = (bf16[4,1280,128]{2,1,0:T(8,128)(2,1)}, bf16[4,1280,128]{2,1,0:T(8,128)(2,1)S(1)}, u32[]{:S(2)}, u32[]{:S(2)}) collective-permute-start(bf16[4,1280,128]{2,1,0:T(8,128)(2,1)} %reduce-scatter.2.cloned.1.call-done), channel_id=1, source_target_pairs={{1,0},{2,1},{3,2},{4,3},{5,4},{6,5},{7,6},{9,8},{10,9},{11,10},{12... | collective-permute-start | bytes 3932168 | tf_op jit(solution)/shard_map/ppermute | solution.py:18
  279.2 74.4 %copy-start.1 = (bf16[4,10,128,128]{3,2,1,0:T(8,128)(2,1)}, bf16[4,10,128,128]{3,2,1,0:T(8,128)(2,1)S(1)}, u32[]{:S(2)}) copy-start(bf16[4,10,128,128]{3,2,1,0:T(8,128)(2,1)S(1)} %copy.14) | copy-start | bytes 3932164
Sparse Core Ops, SparseCore 0:
  60.7 12.8 reduce-scatter.1
  280.4 71.5 all-reduce.1
where the time goes:
time: 363 us; the launch traced here: 360 us
  waiting for transfers between devices  140 us (39%)
  local copies, waits for them, and re-layouts  94.6 us (26%)
  matrix products  84.7 us (23%)
  other arithmetic  21.4 us (6%)
  between operations  14.1 us (4%)
  starting transfers between devices  5.14 us (1%)
    dot_general x20, matrix products, add_slot(): jnp.einsum('bij,mbjc->mbic', tiles, chosen, preferred_element_type=jnp.fl...  80.2 us
    psum x1, waiting for transfers between devices, local(): reduced = lax.psum(term, 'rows')  71.7 us
    gather x20, local copies, waits for them, and re-layouts, add_slot(): chosen = jnp.take(panel_blocks, columns_now, axis=1)  58.2 us
    ppermute x1, waiting for transfers between devices, with_halo(): lax.ppermute(lax.slice_in_dim(block, block.shape[dim] - width, None, axis...  55.3 us
    reduce_scatter x1, waiting for transfers between devices, local(): lax.psum_scatter(partial_value.astype(jnp.bfloat16), 'quad', scatter_dime...  13 us
    reshape x1, local copies, waits for them, and re-layouts, local(): jnp.concatenate([solutions[:, :, :width], solutions[:, :, width:]], axis=0)  11 us
    concatenate x1, other arithmetic, local(): jnp.concatenate([solutions[:, :, :width], solutions[:, :, width:]], axis=0)  10.4 us
    slice x1, local copies, waits for them, and re-layouts, local(): solutions[:, :, :width]  9.61 us
  transfers between devices with their start and end apart: 4, of which 3 were waited for; matrix products, arithmetic and copies ran while one was open for 0% of the time, Pallas kernels for 0%

commit v1 on v0

--- a/solution.py
+++ b/solution.py
@@ -63,7 +63,8 @@
     accum = lax.fori_loop(0, mass_blocks.shape[1], add_slot, start)
     mass_applied = accum.astype(jnp.bfloat16).reshape(owned, rows_here, 2 * width)
     term = jnp.einsum("nl,mnc->mlc", sources, mass_applied, preferred_element_type=jnp.float32)
-    reduced = lax.psum(term, "rows")
+    terms = lax.all_gather(term, "rows", axis=0, tiled=False)
+    reduced = terms.sum(axis=0)
     return (mass_applied, reduced)
 
 

time: 363 us -> 333 us (0.917)
  waiting for transfers between devices: 140 us -> 110 us
    psum x1 -> x0, waiting for transfers between devices: 71.7 us -> none  [local(): reduced = lax.psum(term, 'rows')]
    all_gather x0 -> x1, waiting for transfers between devices: none -> 42.1 us  [local(): terms = lax.all_gather(term, 'rows', axis=0, tiled=False)]
where the time goes in v1:
time: 333 us; the launch traced here: 331 us
  waiting for transfers between devices  110 us (33%)
  local copies, waits for them, and re-layouts  93 us (28%)
  matrix products  84.7 us (25%)
  other arithmetic  23.3 us (7%)
  between operations  14.1 us (4%)
  starting transfers between devices  5.14 us (2%)
    dot_general x20, matrix products, add_slot(): jnp.einsum('bij,mbjc->mbic', tiles, chosen, preferred_element_type=jnp.fl...  80.2 us
    gather x20, local copies, waits for them, and re-layouts, add_slot(): chosen = jnp.take(panel_blocks, columns_now, axis=1)  58.2 us
    ppermute x1, waiting for transfers between devices, with_halo(): lax.ppermute(lax.slice_in_dim(block, block.shape[dim] - width, None, axis...  55.3 us
    all_gather x1, waiting for transfers between devices, local(): terms = lax.all_gather(term, 'rows', axis=0, tiled=False)  42.1 us
    reduce_scatter x1, waiting for transfers between devices, local(): lax.psum_scatter(partial_value.astype(jnp.bfloat16), 'quad', scatter_dime...  13 us
    reshape x1, local copies, waits for them, and re-layouts, local(): jnp.concatenate([solutions[:, :, :width], solutions[:, :, width:]], axis=0)  11 us
    concatenate x1, other arithmetic, local(): jnp.concatenate([solutions[:, :, :width], solutions[:, :, width:]], axis=0)  10.4 us
    slice x1, local copies, waits for them, and re-layouts, local(): solutions[:, :, :width]  9.61 us
  transfers between devices with their start and end apart: 4, of which 3 were waited for; matrix products, arithmetic and copies ran while one was open for 0% of the time, Pallas kernels for 0%

profile of v1, /device:TPU:0, one launch (start us, length us, event | category | flops | bytes accessed | tf_op | source)
XLA Modules:
  0.0 331.2 jit_solution(13735670911149692483)
XLA Ops:
  8.2 9.6 %fusion.22 = (bf16[16,1280,64]{2,1,0:T(8,128)(2,1)}, bf16[16,1280,64]{2,1,0:T(8,128)(2,1)}) fusion(bf16[16,1280,128]{2,1,0:T(8,128)(2,1)} %param.7), kind=kLoop, calls=%fused_computation.37 | loop fusion | bytes 10485760 | tf_op jit(solution)/shard_map/slice | solution.py:38
  17.8 10.4 %pad_maximum_fusion = bf16[32,1280,64]{2,1,0:T(8,128)(2,1)} fusion(bf16[16,1280,64]{2,1,0:T(8,128)(2,1)} %get-tuple-element.143, bf16[16,1280,64]{2,1,0:T(8,128)(2,1)} %get-tuple-element.142), kind=kLoop, calls=%fused_computation.14 | loop fusion | flops 2621440 | bytes 10485760 | tf_op jit(solution)/shard_map/concatenate | solution.py:38
  28.2 11.0 %reshape.29 = bf16[32,81920]{1,0:T(8,128)(2,1)} reshape(bf16[32,1280,64]{2,1,0:T(8,128)(2,1)} %pad_maximum_fusion) | data formatting | bytes 10485760 | tf_op jit(solution)/shard_map/reshape | solution.py:38
  39.2 3.4 %convolution_convert_fusion = bf16[16,81920]{1,0:T(8,128)(2,1)S(1)} fusion(bf16[32,81920]{1,0:T(8,128)(2,1)} %reshape.29, bf16[8,16]{1,0:T(8,128)(2,1)S(1)} %get-tuple-element.147, bf16[8,16]{1,0:T(8,128)(2,1)S(1)} %get-tuple-element.146, bf16[8,16]{1,0:T(8,128)(2,1)S(1)} %fusion.21), kind=kOutput, calls=%fused_computation.13 | convolution fusion | flops 85200896 | bytes 7865088 | tf_op jit(solution)/shard_map/dot_general | solution.py:41
  45.5 3.1 squeeze.20
  48.6 3.0 reshape.46
  51.6 4.3 %squeeze.21 = bf16[8,1280,64]{2,1,0:T(8,128)(2,1)} reshape(bf16[655360]{0:T(1024)(128)(2,1)} %reshape.46) | data formatting | bytes 2621440 | tf_op jit(solution)/shard_map/squeeze | solution.py:44
  55.9 4.7 %pad_maximum_fusion.2 = bf16[8,1280,128]{2,1,0:T(8,128)(2,1)} fusion(bf16[8,1280,64]{2,1,0:T(8,128)(2,1)} %squeeze.21, bf16[8,1280,64]{2,1,0:T(8,128)(2,1)S(1)} %squeeze.20), kind=kLoop, calls=%fused_computation.16 | loop fusion | flops 5242880 | bytes 5242880 | tf_op jit(solution)/shard_map/concatenate | solution.py:44
  60.6 13.0 %reduce-scatter.2.cloned.1.call-done = bf16[4,1280,128]{2,1,0:T(8,128)(2,1)} async-done(((bf16[8,1280,128]{2,1,0:T(8,128)(2,1)}), bf16[4,1280,128]{2,1,0:T(8,128)(2,1)}) %reduce-scatter.2.cloned.1.call-update) | async-done | bytes 1310736 | tf_op jit(solution)/shard_map/reduce_scatter | solution.py:45
  73.6 3.8 %collective-permute-start = (bf16[4,1280,128]{2,1,0:T(8,128)(2,1)}, bf16[4,1280,128]{2,1,0:T(8,128)(2,1)S(1)}, u32[]{:S(2)}, u32[]{:S(2)}) collective-permute-start(bf16[4,1280,128]{2,1,0:T(8,128)(2,1)} %reduce-scatter.2.cloned.1.call-done), channel_id=1, source_target_pairs={{0,1},{1,2},{2,3},{3,4},{4,5},{5,6},{6,7},{8,9},{9,10},{10,11},{11... | collective-permute-start | bytes 3932168 | tf_op jit(solution)/shard_map/ppermute | solution.py:15
  78.8 55.3 %collective-permute-done = bf16[4,1280,128]{2,1,0:T(8,128)(2,1)S(1)} collective-permute-done((bf16[4,1280,128]{2,1,0:T(8,128)(2,1)}, bf16[4,1280,128]{2,1,0:T(8,128)(2,1)S(1)}, u32[]{:S(2)}, u32[]{:S(2)}) %collective-permute-start) | collective-permute-done | bytes 1310752 | tf_op jit(solution)/shard_map/ppermute | solution.py:15
  134.1 3.1 pad_maximum_fusion.1
  137.2 139.2 %while.14 = (s32[]{:T(128)}, f32[4,10,128,128]{2,3,0,1:T(8,128)}, s32[10,20]{0,1:T(8,128)S(1)}, bf16[4,30,128,128]{3,2,1,0:T(8,128)(2,1)}, bf16[10,20,128,128]{3,2,1,0:T(8,128)(2,1)}, /*index=5*/s32[]{:T(128)}, s32[]{:T(128)}) while((s32[]{:T(128)}, f32[4,10,128,128]{2,3,0,1:T(8,128)}, s32[10,20]{0,1:T(8,128)S(1)}, ...), condition=%wide.region_2.3_spmd.clone, body=%wide.region_1.2_spmd.clone.sunk | while | flops 169739328 | bytes 9507599 | solution.py:63
  137.2 2.9 gather_fusion
  140.2 3.2 bitcast_add_fusion.2
  143.4 2.9 gather_fusion
  146.3 4.1 %bitcast_add_fusion.2 = f32[4,10,128,128]{2,3,0,1:T(8,128)} fusion(f32[4,10,128,128]{2,3,0,1:T(8,128)} %get-tuple-element.191, bf16[10,4,128,128]{3,2,1,0:T(8,128)(2,1)S(1)} %gather_fusion, pred[10]{0:T(512)(128)(4,1)S(1)} %get-tuple-element.182, pred[]{:T(512)S(6)} %compare.3, bf16[10,20,128,128]{3,2,1,0:T(8,128)(2,1)} %get-tuple-element.201, ...), kind=kOutput, calls=%fused_computation.1.clone.1 | convolution fusion | flops 169738240 | bytes 6881803 | tf_op jit(solution)/shard_map/while/body/eval_jaxpr/bij,mbjc->mbic/dot_general | solution.py:58
  150.4 2.9 gather_fusion
  153.3 4.1 %bitcast_add_fusion.2 = f32[4,10,128,128]{2,3,0,1:T(8,128)} fusion(f32[4,10,128,128]{2,3,0,1:T(8,128)} %get-tuple-element.191, bf16[10,4,128,128]{3,2,1,0:T(8,128)(2,1)S(1)} %gather_fusion, pred[10]{0:T(512)(128)(4,1)S(1)} %get-tuple-element.182, pred[]{:T(512)S(6)} %compare.3, bf16[10,20,128,128]{3,2,1,0:T(8,128)(2,1)} %get-tuple-element.201, ...), kind=kOutput, calls=%fused_computation.1.clone.1 | convolution fusion | flops 169738240 | bytes 6881803 | tf_op jit(solution)/shard_map/while/body/eval_jaxpr/bij,mbjc->mbic/dot_general | solution.py:58
  157.4 2.9 gather_fusion
  160.3 4.1 %bitcast_add_fusion.2 = f32[4,10,128,128]{2,3,0,1:T(8,128)} fusion(f32[4,10,128,128]{2,3,0,1:T(8,128)} %get-tuple-element.191, bf16[10,4,128,128]{3,2,1,0:T(8,128)(2,1)S(1)} %gather_fusion, pred[10]{0:T(512)(128)(4,1)S(1)} %get-tuple-element.182, pred[]{:T(512)S(6)} %compare.3, bf16[10,20,128,128]{3,2,1,0:T(8,128)(2,1)} %get-tuple-element.201, ...), kind=kOutput, calls=%fused_computation.1.clone.1 | convolution fusion | flops 169738240 | bytes 6881803 | tf_op jit(solution)/shard_map/while/body/eval_jaxpr/bij,mbjc->mbic/dot_general | solution.py:58
  164.4 2.9 gather_fusion
  167.3 4.1 %bitcast_add_fusion.2 = f32[4,10,128,128]{2,3,0,1:T(8,128)} fusion(f32[4,10,128,128]{2,3,0,1:T(8,128)} %get-tuple-element.191, bf16[10,4,128,128]{3,2,1,0:T(8,128)(2,1)S(1)} %gather_fusion, pred[10]{0:T(512)(128)(4,1)S(1)} %get-tuple-element.182, pred[]{:T(512)S(6)} %compare.3, bf16[10,20,128,128]{3,2,1,0:T(8,128)(2,1)} %get-tuple-element.201, ...), kind=kOutput, calls=%fused_computation.1.clone.1 | convolution fusion | flops 169738240 | bytes 6881803 | tf_op jit(solution)/shard_map/while/body/eval_jaxpr/bij,mbjc->mbic/dot_general | solution.py:58
  171.4 2.9 gather_fusion
  174.3 4.1 %bitcast_add_fusion.2 = f32[4,10,128,128]{2,3,0,1:T(8,128)} fusion(f32[4,10,128,128]{2,3,0,1:T(8,128)} %get-tuple-element.191, bf16[10,4,128,128]{3,2,1,0:T(8,128)(2,1)S(1)} %gather_fusion, pred[10]{0:T(512)(128)(4,1)S(1)} %get-tuple-element.182, pred[]{:T(512)S(6)} %compare.3, bf16[10,20,128,128]{3,2,1,0:T(8,128)(2,1)} %get-tuple-element.201, ...), kind=kOutput, calls=%fused_computation.1.clone.1 | convolution fusion | flops 169738240 | bytes 6881803 | tf_op jit(solution)/shard_map/while/body/eval_jaxpr/bij,mbjc->mbic/dot_general | solution.py:58
  178.4 2.9 gather_fusion
  181.3 4.1 %bitcast_add_fusion.2 = f32[4,10,128,128]{2,3,0,1:T(8,128)} fusion(f32[4,10,128,128]{2,3,0,1:T(8,128)} %get-tuple-element.191, bf16[10,4,128,128]{3,2,1,0:T(8,128)(2,1)S(1)} %gather_fusion, pred[10]{0:T(512)(128)(4,1)S(1)} %get-tuple-element.182, pred[]{:T(512)S(6)} %compare.3, bf16[10,20,128,128]{3,2,1,0:T(8,128)(2,1)} %get-tuple-element.201, ...), kind=kOutput, calls=%fused_computation.1.clone.1 | convolution fusion | flops 169738240 | bytes 6881803 | tf_op jit(solution)/shard_map/while/body/eval_jaxpr/bij,mbjc->mbic/dot_general | solution.py:58
  185.4 2.9 gather_fusion
  188.3 4.1 %bitcast_add_fusion.2 = f32[4,10,128,128]{2,3,0,1:T(8,128)} fusion(f32[4,10,128,128]{2,3,0,1:T(8,128)} %get-tuple-element.191, bf16[10,4,128,128]{3,2,1,0:T(8,128)(2,1)S(1)} %gather_fusion, pred[10]{0:T(512)(128)(4,1)S(1)} %get-tuple-element.182, pred[]{:T(512)S(6)} %compare.3, bf16[10,20,128,128]{3,2,1,0:T(8,128)(2,1)} %get-tuple-element.201, ...), kind=kOutput, calls=%fused_computation.1.clone.1 | convolution fusion | flops 169738240 | bytes 6881803 | tf_op jit(solution)/shard_map/while/body/eval_jaxpr/bij,mbjc->mbic/dot_general | solution.py:58
  192.4 2.9 gather_fusion
  195.3 4.1 %bitcast_add_fusion.2 = f32[4,10,128,128]{2,3,0,1:T(8,128)} fusion(f32[4,10,128,128]{2,3,0,1:T(8,128)} %get-tuple-element.191, bf16[10,4,128,128]{3,2,1,0:T(8,128)(2,1)S(1)} %gather_fusion, pred[10]{0:T(512)(128)(4,1)S(1)} %get-tuple-element.182, pred[]{:T(512)S(6)} %compare.3, bf16[10,20,128,128]{3,2,1,0:T(8,128)(2,1)} %get-tuple-element.201, ...), kind=kOutput, calls=%fused_computation.1.clone.1 | convolution fusion | flops 169738240 | bytes 6881803 | tf_op jit(solution)/shard_map/while/body/eval_jaxpr/bij,mbjc->mbic/dot_general | solution.py:58
  199.4 2.9 gather_fusion
  202.3 4.1 %bitcast_add_fusion.2 = f32[4,10,128,128]{2,3,0,1:T(8,128)} fusion(f32[4,10,128,128]{2,3,0,1:T(8,128)} %get-tuple-element.191, bf16[10,4,128,128]{3,2,1,0:T(8,128)(2,1)S(1)} %gather_fusion, pred[10]{0:T(512)(128)(4,1)S(1)} %get-tuple-element.182, pred[]{:T(512)S(6)} %compare.3, bf16[10,20,128,128]{3,2,1,0:T(8,128)(2,1)} %get-tuple-element.201, ...), kind=kOutput, calls=%fused_computation.1.clone.1 | convolution fusion | flops 169738240 | bytes 6881803 | tf_op jit(solution)/shard_map/while/body/eval_jaxpr/bij,mbjc->mbic/dot_general | solution.py:58
  206.4 2.9 gather_fusion
  209.3 4.1 %bitcast_add_fusion.2 = f32[4,10,128,128]{2,3,0,1:T(8,128)} fusion(f32[4,10,128,128]{2,3,0,1:T(8,128)} %get-tuple-element.191, bf16[10,4,128,128]{3,2,1,0:T(8,128)(2,1)S(1)} %gather_fusion, pred[10]{0:T(512)(128)(4,1)S(1)} %get-tuple-element.182, pred[]{:T(512)S(6)} %compare.3, bf16[10,20,128,128]{3,2,1,0:T(8,128)(2,1)} %get-tuple-element.201, ...), kind=kOutput, calls=%fused_computation.1.clone.1 | convolution fusion | flops 169738240 | bytes 6881803 | tf_op jit(solution)/shard_map/while/body/eval_jaxpr/bij,mbjc->mbic/dot_general | solution.py:58
  213.4 2.9 gather_fusion
  216.3 4.1 %bitcast_add_fusion.2 = f32[4,10,128,128]{2,3,0,1:T(8,128)} fusion(f32[4,10,128,128]{2,3,0,1:T(8,128)} %get-tuple-element.191, bf16[10,4,128,128]{3,2,1,0:T(8,128)(2,1)S(1)} %gather_fusion, pred[10]{0:T(512)(128)(4,1)S(1)} %get-tuple-element.182, pred[]{:T(512)S(6)} %compare.3, bf16[10,20,128,128]{3,2,1,0:T(8,128)(2,1)} %get-tuple-element.201, ...), kind=kOutput, calls=%fused_computation.1.clone.1 | convolution fusion | flops 169738240 | bytes 6881803 | tf_op jit(solution)/shard_map/while/body/eval_jaxpr/bij,mbjc->mbic/dot_general | solution.py:58
  220.4 2.9 gather_fusion
  223.4 4.1 %bitcast_add_fusion.2 = f32[4,10,128,128]{2,3,0,1:T(8,128)} fusion(f32[4,10,128,128]{2,3,0,1:T(8,128)} %get-tuple-element.191, bf16[10,4,128,128]{3,2,1,0:T(8,128)(2,1)S(1)} %gather_fusion, pred[10]{0:T(512)(128)(4,1)S(1)} %get-tuple-element.182, pred[]{:T(512)S(6)} %compare.3, bf16[10,20,128,128]{3,2,1,0:T(8,128)(2,1)} %get-tuple-element.201, ...), kind=kOutput, calls=%fused_computation.1.clone.1 | convolution fusion | flops 169738240 | bytes 6881803 | tf_op jit(solution)/shard_map/while/body/eval_jaxpr/bij,mbjc->mbic/dot_general | solution.py:58
  227.4 2.9 gather_fusion
  230.4 4.1 %bitcast_add_fusion.2 = f32[4,10,128,128]{2,3,0,1:T(8,128)} fusion(f32[4,10,128,128]{2,3,0,1:T(8,128)} %get-tuple-element.191, bf16[10,4,128,128]{3,2,1,0:T(8,128)(2,1)S(1)} %gather_fusion, pred[10]{0:T(512)(128)(4,1)S(1)} %get-tuple-element.182, pred[]{:T(512)S(6)} %compare.3, bf16[10,20,128,128]{3,2,1,0:T(8,128)(2,1)} %get-tuple-element.201, ...), kind=kOutput, calls=%fused_computation.1.clone.1 | convolution fusion | flops 169738240 | bytes 6881803 | tf_op jit(solution)/shard_map/while/body/eval_jaxpr/bij,mbjc->mbic/dot_general | solution.py:58
  237.4 4.1 %bitcast_add_fusion.2 = f32[4,10,128,128]{2,3,0,1:T(8,128)} fusion(f32[4,10,128,128]{2,3,0,1:T(8,128)} %get-tuple-element.191, bf16[10,4,128,128]{3,2,1,0:T(8,128)(2,1)S(1)} %gather_fusion, pred[10]{0:T(512)(128)(4,1)S(1)} %get-tuple-element.182, pred[]{:T(512)S(6)} %compare.3, bf16[10,20,128,128]{3,2,1,0:T(8,128)(2,1)} %get-tuple-element.201, ...), kind=kOutput, calls=%fused_computation.1.clone.1 | convolution fusion | flops 169738240 | bytes 6881803 | tf_op jit(solution)/shard_map/while/body/eval_jaxpr/bij,mbjc->mbic/dot_general | solution.py:58
  244.4 4.1 %bitcast_add_fusion.2 = f32[4,10,128,128]{2,3,0,1:T(8,128)} fusion(f32[4,10,128,128]{2,3,0,1:T(8,128)} %get-tuple-element.191, bf16[10,4,128,128]{3,2,1,0:T(8,128)(2,1)S(1)} %gather_fusion, pred[10]{0:T(512)(128)(4,1)S(1)} %get-tuple-element.182, pred[]{:T(512)S(6)} %compare.3, bf16[10,20,128,128]{3,2,1,0:T(8,128)(2,1)} %get-tuple-element.201, ...), kind=kOutput, calls=%fused_computation.1.clone.1 | convolution fusion | flops 169738240 | bytes 6881803 | tf_op jit(solution)/shard_map/while/body/eval_jaxpr/bij,mbjc->mbic/dot_general | solution.py:58
  251.4 4.1 %bitcast_add_fusion.2 = f32[4,10,128,128]{2,3,0,1:T(8,128)} fusion(f32[4,10,128,128]{2,3,0,1:T(8,128)} %get-tuple-element.191, bf16[10,4,128,128]{3,2,1,0:T(8,128)(2,1)S(1)} %gather_fusion, pred[10]{0:T(512)(128)(4,1)S(1)} %get-tuple-element.182, pred[]{:T(512)S(6)} %compare.3, bf16[10,20,128,128]{3,2,1,0:T(8,128)(2,1)} %get-tuple-element.201, ...), kind=kOutput, calls=%fused_computation.1.clone.1 | convolution fusion | flops 169738240 | bytes 6881803 | tf_op jit(solution)/shard_map/while/body/eval_jaxpr/bij,mbjc->mbic/dot_general | solution.py:58
  258.4 4.1 %bitcast_add_fusion.2 = f32[4,10,128,128]{2,3,0,1:T(8,128)} fusion(f32[4,10,128,128]{2,3,0,1:T(8,128)} %get-tuple-element.191, bf16[10,4,128,128]{3,2,1,0:T(8,128)(2,1)S(1)} %gather_fusion, pred[10]{0:T(512)(128)(4,1)S(1)} %get-tuple-element.182, pred[]{:T(512)S(6)} %compare.3, bf16[10,20,128,128]{3,2,1,0:T(8,128)(2,1)} %get-tuple-element.201, ...), kind=kOutput, calls=%fused_computation.1.clone.1 | convolution fusion | flops 169738240 | bytes 6881803 | tf_op jit(solution)/shard_map/while/body/eval_jaxpr/bij,mbjc->mbic/dot_general | solution.py:58
  265.4 4.1 %bitcast_add_fusion.2 = f32[4,10,128,128]{2,3,0,1:T(8,128)} fusion(f32[4,10,128,128]{2,3,0,1:T(8,128)} %get-tuple-element.191, bf16[10,4,128,128]{3,2,1,0:T(8,128)(2,1)S(1)} %gather_fusion, pred[10]{0:T(512)(128)(4,1)S(1)} %get-tuple-element.182, pred[]{:T(512)S(6)} %compare.3, bf16[10,20,128,128]{3,2,1,0:T(8,128)(2,1)} %get-tuple-element.201, ...), kind=kOutput, calls=%fused_computation.1.clone.1 | convolution fusion | flops 169738240 | bytes 6881803 | tf_op jit(solution)/shard_map/while/body/eval_jaxpr/bij,mbjc->mbic/dot_general | solution.py:58
  272.4 4.1 %bitcast_add_fusion.2 = f32[4,10,128,128]{2,3,0,1:T(8,128)} fusion(f32[4,10,128,128]{2,3,0,1:T(8,128)} %get-tuple-element.191, bf16[10,4,128,128]{3,2,1,0:T(8,128)(2,1)S(1)} %gather_fusion, pred[10]{0:T(512)(128)(4,1)S(1)} %get-tuple-element.182, pred[]{:T(512)S(6)} %compare.3, bf16[10,20,128,128]{3,2,1,0:T(8,128)(2,1)} %get-tuple-element.201, ...), kind=kOutput, calls=%fused_computation.1.clone.1 | convolution fusion | flops 169738240 | bytes 6881803 | tf_op jit(solution)/shard_map/while/body/eval_jaxpr/bij,mbjc->mbic/dot_general | solution.py:58
  280.3 42.1 %all-gather.3.cloned.1.call-done = f32[32,64,128]{2,1,0:T(8,128)} async-done(((f32[4,64,128]{2,1,0:T(8,128)}), f32[32,64,128]{2,1,0:T(8,128)}) %all-gather.3.cloned.1.call-update) | async-done | bytes 1048592 | tf_op jit(solution)/shard_map/all_gather | solution.py:66
  (71 shorter events, 28.9 us)
Async XLA Ops:
  7.2 272.0 %copy-start = (bf16[1280,64]{0,1:T(8,128)(2,1)S(1)}, bf16[1280,64]{0,1:T(8,128)(2,1)}, u32[]{:S(2)}) copy-start(bf16[1280,64]{0,1:T(8,128)(2,1)} %param.11) | copy-start | bytes 491524
  7.2 66.4 %reduce-scatter.2.cloned.1.call-start = ((), (), s32[]{:S(2)}) async-start(), calls=%async_computation.1 | async-start | bytes 3932160 | tf_op jit(solution)/shard_map/reduce_scatter | solution.py:45
  60.6 18.2 %copy-start.2 = (s32[10,20]{1,0:T(8,128)S(1)}, s32[10,20]{1,0:T(8,128)}, u32[]{:S(2)}) copy-start(s32[10,20]{1,0:T(8,128)} %param.10) | copy-start | bytes 2404
  60.6 261.9 %all-gather.3.cloned.1.call-start = ((), (), s32[]{:S(2)}) async-start(), calls=%async_computation.2 | async-start | bytes 1179648 | tf_op jit(solution)/shard_map/all_gather | solution.py:66
  73.6 60.5 %collective-permute-start = (bf16[4,1280,128]{2,1,0:T(8,128)(2,1)}, bf16[4,1280,128]{2,1,0:T(8,128)(2,1)S(1)}, u32[]{:S(2)}, u32[]{:S(2)}) collective-permute-start(bf16[4,1280,128]{2,1,0:T(8,128)(2,1)} %reduce-scatter.2.cloned.1.call-done), channel_id=1, source_target_pairs={{0,1},{1,2},{2,3},{3,4},{4,5},{5,6},{6,7},{8,9},{9,10},{10,11},{11... | collective-permute-start | bytes 3932168 | tf_op jit(solution)/shard_map/ppermute | solution.py:15
  77.4 56.7 %collective-permute-start.1 = (bf16[4,1280,128]{2,1,0:T(8,128)(2,1)}, bf16[4,1280,128]{2,1,0:T(8,128)(2,1)S(1)}, u32[]{:S(2)}, u32[]{:S(2)}) collective-permute-start(bf16[4,1280,128]{2,1,0:T(8,128)(2,1)} %reduce-scatter.2.cloned.1.call-done), channel_id=1, source_target_pairs={{1,0},{2,1},{3,2},{4,3},{5,4},{6,5},{7,6},{9,8},{10,9},{11,10},{12... | collective-permute-start | bytes 3932168 | tf_op jit(solution)/shard_map/ppermute | solution.py:18
  279.2 45.2 %copy-start.1 = (bf16[4,10,128,128]{3,2,1,0:T(8,128)(2,1)}, bf16[4,10,128,128]{3,2,1,0:T(8,128)(2,1)S(1)}, u32[]{:S(2)}) copy-start(bf16[4,10,128,128]{3,2,1,0:T(8,128)(2,1)S(1)} %copy.18) | copy-start | bytes 3932164
Sparse Core Ops, SparseCore 0:
  60.7 12.8 reduce-scatter.1
  280.4 41.9 all-gather.2
